TPU v7x, 512 devices: a whole 4x4x16 slice. The times are simulated.
512 devices in a mesh: row: 8 (over y, core), col: 16 (over z), ch: 4 (over x).
Axes of the slice: x: 4, y: 4, z: 16, core: 2. Of those that a mesh axis runs over, the one named last changes fastest.
Arguments:
- image: bfloat16 [256, 32, 2048], P('ch', 'row', 'col'), may hold values from -6 to 6
- depth_kernel: float32 [256, 49], P('ch'), may hold values from -0.875 to 0.875
- norm_gain: float32 [256], P('ch'), may hold values from 0.25 to 1.75
- norm_shift: float32 [256], P('ch'), may hold values from -3 to 3
- expand_weight: bfloat16 [256, 1024], P(None, 'ch'), may hold values from -0.375 to 0.375
- expand_bias: float32 [1024], replicated, may hold values from -3 to 3
- reduce_weight: bfloat16 [1024, 256], P('ch'), may hold values from -0.1875 to 0.1875
- cotangent: bfloat16 [256, 32, 2048], P('ch', 'row', 'col'), may hold values from -6 to 6
Outputs:
- result: bfloat16 [256, 32, 2048], P('ch', 'row', 'col')
- grad_image: bfloat16 [256, 32, 2048], P('ch', 'row', 'col')
- grad_kernel: float32 [256, 49], P('ch')
- grad_gain: float32 [256], P('ch')
- grad_shift: float32 [256], P('ch')
- grad_expand: float32 [256, 1024], P(None, 'ch')
- grad_offset: float32 [1024], P('ch')
- grad_reduce: float32 [1024, 256], P('ch')
All inputs are finite; a program needn't handle non-finite values.
Results may differ from a plain program's by a relative error of at most 0.011.
Values may be sent and summed in bfloat16 or wider, within the bound.
No kernel may reach another device: no remote copies, remote signals or barrier semaphores. Data moves between devices by JAX's collectives and lax.ppermute only.
A program may use at most 64 MiB of HBM per device.

v0:
```python
import jax
import jax.numpy as jnp
from jax import lax
from jax.sharding import PartitionSpec as P

KSIZE = 7
epsilon = 1e-06
root_two_pi = 0.7978845608028654
cubic_coef = 0.044715


def padded_2(x, sides, width):
    for axis, dim in sides:
        size, length = (lax.axis_size(axis), x.shape[dim])
        up = [(i, (i + 1) % size) for i in range(size - 1)]
        down = [(j, i) for i, j in up]
        last = lax.slice_in_dim(x, length - width, length, axis=dim)
        leading = lax.slice_in_dim(x, 0, width, axis=dim)
        before = lax.ppermute(last, axis, up)
        after = lax.ppermute(leading, axis, down)
        x = jnp.concatenate([before, x, after], axis=dim)
    return x


def product(left, right, dims):
    return lax.dot_general(
        left.astype(jnp.float32),
        right.astype(jnp.float32),
        dims,
        preferred_element_type=jnp.float32,
    )


def gelu_pair(hidden):
    inner = root_two_pi * (hidden + cubic_coef * hidden * hidden * hidden)
    tangent = jnp.tanh(inner)
    value = 0.5 * hidden * (1.0 + tangent)
    slope = 0.5 * (1.0 + tangent) + 0.5 * hidden * (1.0 - tangent * tangent) * root_two_pi * (
        1.0 + 3.0 * cubic_coef * hidden * hidden
    )
    return (value, slope)


def tap_window(padded, kernel, tap, first, second, tile_rows, tile_cols):
    window = lax.dynamic_slice(
        padded, (jnp.int32(0), first, second), (padded.shape[0], tile_rows, tile_cols)
    )
    weight = lax.dynamic_slice_in_dim(kernel, tap, 1, 1)
    return weight[:, :, None] * window


def forward_taps(padded, kernel, span, tile_rows, tile_cols):

    def forward_step(tap, accum):
        tap = jnp.asarray(tap).astype(jnp.int32)
        first = tap // span
        second = tap % span
        return accum + tap_window(padded, kernel, tap, first, second, tile_rows, tile_cols)

    accum = jnp.zeros((padded.shape[0], tile_rows, tile_cols), jnp.float32)
    return lax.fori_loop(0, span * span, forward_step, accum)


def backward_taps(padded, kernel, span, tile_rows, tile_cols):
    reach = span - 1

    def backward_step(tap, accum):
        tap = jnp.asarray(tap).astype(jnp.int32)
        first = reach - tap // span
        second = reach - tap % span
        return accum + tap_window(padded, kernel, tap, first, second, tile_rows, tile_cols)

    accum = jnp.zeros((padded.shape[0], tile_rows, tile_cols), jnp.float32)
    return lax.fori_loop(0, span * span, backward_step, accum)


def kernel_grad(grad_mixed, padded, span, tile_rows, tile_cols):

    def kernel_step(tap, table):
        tap = jnp.asarray(tap).astype(jnp.int32)
        first = tap // span
        second = tap % span
        window = lax.dynamic_slice(
            padded, (jnp.int32(0), first, second), (padded.shape[0], tile_rows, tile_cols)
        )
        column = jnp.sum(grad_mixed * window, axis=(1, 2))
        return lax.dynamic_update_slice_in_dim(table, column[:, None], tap, 1)

    table = jnp.zeros((grad_mixed.shape[0], span * span), jnp.float32)
    return lax.fori_loop(0, span * span, kernel_step, table)


def body(
    image, depth_kernel, norm_gain, norm_shift, expand_weight, expand_bias, reduce_weight, cotangent
):
    channels, tile_rows, tile_cols = image.shape
    pixels = tile_rows * tile_cols
    all_channels = channels * lax.axis_size("ch")
    hid_local = reduce_weight.shape[0]
    half = KSIZE // 2
    padded = padded_2(image, (("row", 1), ("col", 2)), half).astype(jnp.float32)
    mixed = forward_taps(padded, depth_kernel, KSIZE, tile_rows, tile_cols)
    flat_cot = cotangent.reshape(channels, pixels)
    contract_first = (((0,), (0,)), ((), ()))
    contract_last = (((1,), (1,)), ((), ()))
    plain = (((1,), (0,)), ((), ()))
    centre = lax.psum(jnp.sum(mixed, axis=0), "ch") / all_channels
    diff = mixed - centre
    variance = lax.psum(jnp.sum(diff * diff, axis=0), "ch") / all_channels
    inverse = lax.rsqrt(variance + epsilon)
    normed = diff * inverse
    normal = (normed * norm_gain[:, None, None] + norm_shift[:, None, None]).astype(jnp.bfloat16)
    flat_normal = normal.reshape(channels, pixels)
    bias_local = lax.dynamic_slice_in_dim(expand_bias, lax.axis_index("ch") * hid_local, hid_local)
    full_normal = lax.all_gather(flat_normal, "ch", axis=0, tiled=True)
    hidden = product(expand_weight, full_normal, contract_first) + bias_local[:, None]
    value, slope = gelu_pair(hidden)
    active = value.astype(jnp.bfloat16)
    mlp_local = lax.psum_scatter(
        product(reduce_weight, active, contract_first), "ch", scatter_dimension=0, tiled=True
    )
    full_cot = lax.all_gather(flat_cot, "ch", axis=0, tiled=True)
    grad_act = product(reduce_weight, full_cot, plain)
    grad_hidden = (grad_act * slope).astype(jnp.bfloat16)
    grad_red = product(active, full_cot, contract_last)
    grad_exp = product(full_normal, grad_hidden, contract_last)
    grad_off = jnp.sum(grad_hidden.astype(jnp.float32), axis=1)
    grad_local = lax.psum_scatter(
        product(expand_weight, grad_hidden, plain).astype(jnp.bfloat16),
        "ch",
        scatter_dimension=0,
        tiled=True,
    ).astype(jnp.float32)
    grad_normal = grad_local.reshape(channels, tile_rows, tile_cols)
    grad_normed = grad_normal * norm_gain[:, None, None]
    plain_sum, cross_sum = lax.psum(
        (jnp.sum(grad_normed, axis=0), jnp.sum(grad_normed * normed, axis=0)), "ch"
    )
    grad_gain = jnp.sum(grad_normal * normed, axis=(1, 2))
    grad_shift = jnp.sum(grad_normal, axis=(1, 2))
    grad_mixed = inverse * (
        grad_normed - plain_sum / all_channels - normed * (cross_sum / all_channels)
    )
    result = (image.astype(jnp.float32) + mlp_local.reshape(channels, tile_rows, tile_cols)).astype(
        jnp.bfloat16
    )
    grad_pad = padded_2(grad_mixed.astype(jnp.bfloat16), (("row", 1), ("col", 2)), half).astype(
        grad_mixed.dtype
    )
    grad_image = (
        cotangent.astype(jnp.float32)
        + backward_taps(grad_pad, depth_kernel, KSIZE, tile_rows, tile_cols)
    ).astype(jnp.bfloat16)
    grad_kernel = kernel_grad(grad_mixed, padded, KSIZE, tile_rows, tile_cols)
    totals = lax.psum(
        (grad_kernel, grad_gain, grad_shift, grad_exp, grad_off, grad_red), ("row", "col")
    )
    pixels_all = pixels * lax.axis_size("row") * lax.axis_size("col")
    scale = float(pixels_all) ** (-0.5)
    return (
        result,
        grad_image,
        totals[0] * scale,
        totals[1] * scale,
        totals[2] * scale,
        totals[3] * scale,
        totals[4] * scale,
        totals[5] * scale,
    )


def solution(mesh):
    in_specs = (
        P("ch", "row", "col"),
        P("ch", None),
        P("ch"),
        P("ch"),
        P(None, "ch"),
        P(),
        P("ch", None),
        P("ch", "row", "col"),
    )
    out_specs = (
        P("ch", "row", "col"),
        P("ch", "row", "col"),
        P("ch", None),
        P("ch"),
        P("ch"),
        P(None, "ch"),
        P("ch"),
        P("ch", None),
    )
    return jax.shard_map(body, mesh=mesh, in_specs=in_specs, out_specs=out_specs, check_vma=False)
```

profile of v0, /device:TPU:1, one launch (start us, length us, event | category | flops | bytes accessed | tf_op | source)
XLA Modules:
  0.0 1113.7 jit_solution(2712978404241594079)
XLA Ops:
  8.1 1.0 fusion.13
  9.0 4.6 collective-permute-start
  13.6 5.5 collective-permute-start.1
  20.3 2.8 collective-permute-start.2
  23.1 1.3 collective-permute-start.3
  24.4 10.6 all_gather.7
  36.5 57.9 %while.48 = (s32[]{:T(128)}, f32[64,4,128]{2,1,0:T(4,128)S(1)}, f32[64,49]{0,1:T(8,128)}, f32[64,10,134]{2,1,0:T(8,128)S(1)}, s32[]{:T(128)}, /*index=5*/s32[]{:T(128)}, s32[]{:T(128)}, s32[]{:T(128)}, s32[]{:T(128)}, s32[]{:T(128)}) while((s32[]{:T(128)}, f32[64,4,128]{2,1,0:T(4,128)S(1)}, f32[64,49]{0,1:T(8,128)}, ...), condition=%wide.region_1.2_spmd.clone, body=%wide.region_0.1_spmd.clone.sunk | while | flops 98325 | bytes 394290 | solution.py:61
  94.4 7.8 psum.70
  102.4 6.0 psum.71
  109.3 10.1 all_gather.6
  119.6 1.1 fusion.8
  123.7 1.0 copy.25
  124.7 346.0 %all-reduce.5.cloned.1.call-done = (f32[256,256]{1,0:T(8,128)}, f32[256,256]{1,0:T(8,128)}) async-done(((f32[256,256]{1,0:T(8,128)}, f32[256,256]{1,0:T(8,128)}), (f32[256,256]{1,0:T(8,128)}, f32[256,256]{1,0:T(8,128)})) %all-reduce.5.cloned.1.call-update) | async-done | bytes 524304 | tf_op jit(solution)/shard_map/psum | solution.py:155
  470.8 1.9 broadcast_multiply_fusion
  472.6 1.0 copy.28
  474.4 8.4 all-reduce.2
  482.9 50.7 %while.47 = (s32[]{:T(128)}, f32[64,49]{0,1:T(8,128)S(1)}, f32[64,10,134]{2,1,0:T(8,128)S(1)}, f32[64,4,128]{2,1,0:T(4,128)S(1)}, s32[]{:T(128)}, /*index=5*/s32...) while((s32[]{:T(128)}, f32[64,49]{0,1:T(8,128)S(1)}, f32[64,10,134]{2,1,0:T(8,128)S(1)}, ...), condition=%wide.region_16.17_spmd, body=%wide.region_14.16_spmd.sunk | while | flops 65492 | bytes 263208 | solution.py:90
  483.0 0.9 multiply_reduce_fusion.6
  484.0 0.9 multiply_reduce_fusion.6
  485.1 0.9 multiply_reduce_fusion.6
  489.2 0.9 multiply_reduce_fusion.6
  490.2 0.9 multiply_reduce_fusion.6
  491.3 0.9 multiply_reduce_fusion.6
  496.5 0.9 multiply_reduce_fusion.6
  497.5 0.9 multiply_reduce_fusion.6
  502.7 0.9 multiply_reduce_fusion.6
  503.7 0.9 multiply_reduce_fusion.6
  504.7 0.9 multiply_reduce_fusion.6
  508.9 0.9 multiply_reduce_fusion.6
  509.9 0.9 multiply_reduce_fusion.6
  510.9 0.9 multiply_reduce_fusion.6
  516.1 0.9 multiply_reduce_fusion.6
  517.1 0.9 multiply_reduce_fusion.6
  522.3 0.9 multiply_reduce_fusion.6
  523.4 0.9 multiply_reduce_fusion.6
  524.4 0.9 multiply_reduce_fusion.6
  528.5 0.9 multiply_reduce_fusion.6
  529.6 0.9 multiply_reduce_fusion.6
  530.6 0.9 multiply_reduce_fusion.6
  533.7 477.5 %all-reduce = (f32[64,49]{0,1:T(8,128)S(1)}, f32[64]{0:T(128)S(1)}, f32[64]{0:T(128)S(1)}, f32[256]{0:T(256)S(1)}) all-reduce(f32[64,49]{0,1:T(8,128)S(1)} %get-tuple-element.351, f32[64]{0:T(128)S(1)} %get-tuple-element.382, f32[64]{0:T(128)S(1)} %get-tuple-element.384, ...), channel_id=1, replica_groups=mesh['row'=8,'col'=16,'ch'=4] {'row','col'}, use_global_device_ids=true, to_apply=%region_17.18 | all-reduce | flops 3520 | bytes 28160 | tf_op jit(solution)/shard_map/psum | solution.py:155
  1012.4 1.9 collective-permute-start.4
  1014.3 19.1 %collective-permute-start.5 = (bf16[64,3,128]{2,1,0:T(4,128)(2,1)S(1)}, bf16[64,3,128]{2,1,0:T(4,128)(2,1)S(1)}, u32[]{:S(2)}, u32[]{:S(2)}) collective-permute-start(bf16[64,3,128]{2,1,0:T(4,128)(2,1)S(1)} %get-tuple-element.425), channel_id=1, source_target_pairs={{64,0},{128,64},{192,128},{256,192},{320,256},{384,320},{448,384},... | collective-permute-start | bytes 147464 | tf_op jit(solution)/shard_map/ppermute | solution.py:20
  1034.6 1.3 collective-permute-start.6
  1035.9 1.3 collective-permute-start.7
  1037.7 3.5 collective-permute-done.6
  1041.2 3.8 collective-permute-done.7
  1045.8 57.9 %while.49 = (s32[]{:T(128)}, f32[64,4,128]{2,1,0:T(4,128)S(1)}, f32[64,49]{0,1:T(8,128)}, f32[64,10,134]{2,1,0:T(8,128)S(1)}, s32[]{:T(128)}, /*index=5*/s32[]{:...) while((s32[]{:T(128)}, f32[64,4,128]{2,1,0:T(4,128)S(1)}, ...), condition=%wide.region_13.14_spmd.clone, body=%wide.region_12.13_spmd.clone.sunk | while | flops 98327 | bytes 394322 | solution.py:74
  1104.4 1.0 copy.26
  (334 shorter events, 150.6 us)
Async XLA Ops:
  8.0 112.7 %copy-start = (bf16[256,256]{1,0:T(8,128)(2,1)S(1)}, bf16[256,256]{1,0:T(8,128)(2,1)}, u32[]{:S(2)}) copy-start(bf16[256,256]{1,0:T(8,128)(2,1)} %param.20) | copy-start | bytes 393220
  8.0 11.1 copy-start.3
  8.0 462.7 %all-reduce.5.cloned.1.call-start = ((), (), s32[]{:S(2)}) async-start(), calls=%async_computation.4 | async-start | bytes 1048576 | tf_op jit(solution)/shard_map/psum | solution.py:155
  9.0 10.1 collective-permute-start
  13.6 6.3 collective-permute-start.1
  19.1 0.9 copy-start.1
  20.3 15.5 %collective-permute-start.2 = (bf16[64,10,3]{2,1,0:T(8,128)(2,1)S(1)}, bf16[64,10,3]{2,1,0:T(8,128)(2,1)S(1)}, u32[]{:S(2)}, u32[]{:S(2)}) collective-permute-start(bf16[64,10,3]{2,1,0:T(8,128)(2,1)S(1)} %get-tuple-element.422), channel_id=1, source_target_pairs={{0,4},{4,8},{8,12},{12,16},{16,20},{20,24},{24,28},{28,32},{32,36}... | collective-permute-start | bytes 11528 | tf_op jit(solution)/shard_map/ppermute | solution.py:19
  23.1 12.7 %collective-permute-start.3 = (bf16[64,10,3]{2,1,0:T(8,128)(2,1)S(1)}, bf16[64,10,3]{2,1,0:T(8,128)(2,1)S(1)}, u32[]{:S(2)}, u32[]{:S(2)}) collective-permute-start(bf16[64,10,3]{2,1,0:T(8,128)(2,1)S(1)} %get-tuple-element.423), channel_id=1, source_target_pairs={{4,0},{8,4},{12,8},{16,12},{20,16},{24,20},{28,24},{32,28},{36,32}... | collective-permute-start | bytes 11528 | tf_op jit(solution)/shard_map/ppermute | solution.py:20
  108.4 0.7 copy-start.4
  108.4 0.7 copy-start.5
  109.3 10.1 copy-start.2
  122.1 350.5 %reduce-scatter.9.cloned.1.call-start = ((), (), s32[]{:S(2)}) async-start(), calls=%async_computation.3 | async-start | bytes 327680
  123.3 981.1 %reduce-scatter.7.cloned.1.call-start = ((), (), s32[]{:S(2)}) async-start(), calls=%async_computation.2 | async-start | bytes 655360
  1012.4 21.6 %collective-permute-start.4 = (bf16[64,3,128]{2,1,0:T(4,128)(2,1)S(1)}, bf16[64,3,128]{2,1,0:T(4,128)(2,1)S(1)}, u32[]{:S(2)}, u32[]{:S(2)}) collective-permute-start(bf16[64,3,128]{2,1,0:T(4,128)(2,1)S(1)} %get-tuple-element.424), channel_id=1, source_target_pairs={{0,64},{64,128},{128,192},{192,256},{256,320},{320,384},{384,448},... | collective-permute-start | bytes 147464 | tf_op jit(solution)/shard_map/ppermute | solution.py:19
  1014.3 20.0 %collective-permute-start.5 = (bf16[64,3,128]{2,1,0:T(4,128)(2,1)S(1)}, bf16[64,3,128]{2,1,0:T(4,128)(2,1)S(1)}, u32[]{:S(2)}, u32[]{:S(2)}) collective-permute-start(bf16[64,3,128]{2,1,0:T(4,128)(2,1)S(1)} %get-tuple-element.425), channel_id=1, source_target_pairs={{64,0},{128,64},{192,128},{256,192},{320,256},{384,320},{448,384},... | collective-permute-start | bytes 147464 | tf_op jit(solution)/shard_map/ppermute | solution.py:20
  1034.6 6.7 collective-permute-start.6
  1035.9 9.2 collective-permute-start.7
Sparse Core Ops, SparseCore 0:
  122.3 348.4 all-reduce.4
Sparse Core Ops, SparseCore 1:
  125.4 38.8 reduce-scatter.8
  167.0 28.9 reduce-scatter.6
where the time goes:
time: 1120 us; the launch traced here: 1110 us
  blocking collectives  520 us (46%)
  waiting for transfers between devices  355 us (32%)
  other arithmetic  97.2 us (9%)
  local copies, waits for them, and re-layouts  76.4 us (7%)
  starting transfers between devices  37.9 us (3%)
  between operations  15.7 us (1%)
    psum x1, blocking collectives, body(): lax.psum((grad_kernel, grad_gain, grad_shift, grad_exp, grad_off, grad_re...  477 us
    psum x1, waiting for transfers between devices, body(): lax.psum((grad_kernel, grad_gain, grad_shift, grad_exp, grad_off, grad_re...  346 us
    mul x98, local copies, waits for them, and re-layouts, tap_window(): return weight[:, :, None] * window  68.2 us
    reduce_sum x49, other arithmetic, kernel_step(): column = jnp.sum(grad_mixed * window, axis=(1, 2))  46.4 us
    ppermute x4, starting transfers between devices, padded_2(): after = lax.ppermute(leading, axis, down)  27.1 us
  transfers between devices with their start and end apart: 11, of which 5 were waited for; matrix products, arithmetic and copies ran while one was open for 10% of the time, Pallas kernels for 0%

commit v1 on v0

--- a/solution.py
+++ b/solution.py
@@ -153,7 +153,7 @@
     ).astype(jnp.bfloat16)
     grad_kernel = kernel_grad(grad_mixed, padded, KSIZE, tile_rows, tile_cols)
     totals = lax.psum(
-        (grad_kernel, grad_gain, grad_shift, grad_exp, grad_off, grad_red), ("row", "col")
+        lax.psum((grad_kernel, grad_gain, grad_shift, grad_exp, grad_off, grad_red), "row"), "col"
     )
     pixels_all = pixels * lax.axis_size("row") * lax.axis_size("col")
     scale = float(pixels_all) ** (-0.5)

time: 1120 us -> 451 us (0.40)
  blocking collectives: 520 us -> 115 us
  waiting for transfers between devices: 355 us -> 96.9 us
    psum x1, blocking collectives: 477 us -> 24.9 us  [body(): lax.psum((grad_kernel, grad_gain, grad_shift, grad_exp, grad_off, grad_re...]
    psum x1, waiting for transfers between devices: 346 us -> 86.5 us  [body(): lax.psum((grad_kernel, grad_gain, grad_shift, grad_exp, grad_off, grad_re...]
    psum x0 -> x1, blocking collectives: none -> 47.9 us  [body(): lax.psum(lax.psum((grad_kernel, grad_gain, grad_shift, grad_exp, grad_off...]
    ppermute x4, starting transfers between devices: 27.1 us -> 11.3 us  [padded_2(): after = lax.ppermute(leading, axis, down)]
    ppermute x4, starting transfers between devices: 10.6 us -> 21.9 us  [padded_2(): before = lax.ppermute(last, axis, up)]
  transfers between devices with their start and end apart: 11 -> 12, of which waited for: 5 -> 5; matrix products, arithmetic and copies ran while one was open for 10% -> 26% of each run, Pallas kernels for 0% -> 0%
where the time goes in v1:
time: 451 us; the launch traced here: 446 us
  blocking collectives  115 us (25%)
  other arithmetic  97.2 us (22%)
  waiting for transfers between devices  96.9 us (21%)
  local copies, waits for them, and re-layouts  76.4 us (17%)
  starting transfers between devices  33.3 us (7%)
  between operations  15.8 us (4%)
  loops' own time  8.1 us (2%)
    psum x1, waiting for transfers between devices, body(): lax.psum((grad_kernel, grad_gain, grad_shift, grad_exp, grad_off, grad_re...  86.5 us
    mul x98, local copies, waits for them, and re-layouts, tap_window(): return weight[:, :, None] * window  68.2 us
    psum x1, blocking collectives, body(): lax.psum(lax.psum((grad_kernel, grad_gain, grad_shift, grad_exp, grad_off...  47.9 us
    reduce_sum x49, other arithmetic, kernel_step(): column = jnp.sum(grad_mixed * window, axis=(1, 2))  46.4 us
    psum x1, blocking collectives, body(): lax.psum((grad_kernel, grad_gain, grad_shift, grad_exp, grad_off, grad_re...  24.9 us
    ppermute x4, starting transfers between devices, padded_2(): before = lax.ppermute(last, axis, up)  21.9 us
    add x49, other arithmetic, forward_step(): accum + tap_window(padded, kernel, tap, first, second, tile_rows, tile_cols)  21.2 us
    add x49, other arithmetic, backward_step(): accum + tap_window(padded, kernel, tap, first, second, tile_rows, tile_cols)  21.2 us
  transfers between devices with their start and end apart: 12, of which 5 were waited for; matrix products, arithmetic and copies ran while one was open for 26% of the time, Pallas kernels for 0%

profile of v1, /device:TPU:1, one launch (start us, length us, event | category | flops | bytes accessed | tf_op | source)
XLA Modules:
  0.0 446.1 jit_solution(630205602618956242)
XLA Ops:
  8.1 1.0 fusion.13
  9.0 4.6 %collective-permute-start = (bf16[64,3,128]{2,1,0:T(4,128)(2,1)S(1)}, bf16[64,3,128]{2,1,0:T(4,128)(2,1)S(1)}, u32[]{:S(2)}, u32[]{:S(2)}) collective-permute-start(bf16[64,3,128]{2,1,0:T(4,128)(2,1)S(1)} %get-tuple-element.432), channel_id=1, source_target_pairs={{0,64},{64,128},{128,192},{192,256},{256,320},{320,384},{384,448},... | collective-permute-start | bytes 147464 | tf_op jit(solution)/shard_map/ppermute | solution.py:19
  13.6 5.5 %collective-permute-start.1 = (bf16[64,3,128]{2,1,0:T(4,128)(2,1)S(1)}, bf16[64,3,128]{2,1,0:T(4,128)(2,1)S(1)}, u32[]{:S(2)}, u32[]{:S(2)}) collective-permute-start(bf16[64,3,128]{2,1,0:T(4,128)(2,1)S(1)} %get-tuple-element.433), channel_id=1, source_target_pairs={{64,0},{128,64},{192,128},{256,192},{320,256},{384,320},{448,384},... | collective-permute-start | bytes 147464 | tf_op jit(solution)/shard_map/ppermute | solution.py:20
  20.3 2.8 collective-permute-start.2
  23.1 1.3 collective-permute-start.3
  24.4 10.6 %all_gather.7 = bf16[256,512]{1,0:T(8,128)(2,1)S(1)} all-gather(bf16[64,512]{1,0:T(8,128)(2,1)S(1)} %bitcast.43), channel_id=1, replica_groups=mesh['row'=8,'col'=16,'ch'=4] {'ch'}, dimensions={0}, use_global_device_ids=true | all-gather | bytes 327680 | tf_op jit(solution)/shard_map/all_gather | solution.py:122
  36.5 57.9 %while.48 = (s32[]{:T(128)}, f32[64,4,128]{2,1,0:T(4,128)S(1)}, f32[64,49]{0,1:T(8,128)}, f32[64,10,134]{2,1,0:T(8,128)S(1)}, s32[]{:T(128)}, /*index=5*/s32[]{:T(128)}, s32[]{:T(128)}, s32[]{:T(128)}, s32[]{:T(128)}, s32[]{:T(128)}) while((s32[]{:T(128)}, f32[64,4,128]{2,1,0:T(4,128)S(1)}, f32[64,49]{0,1:T(8,128)}, ...), condition=%wide.region_1.2_spmd.clone, body=%wide.region_0.1_spmd.clone.sunk | while | flops 98325 | bytes 394290 | solution.py:61
  94.4 7.8 %psum.112 = f32[4,128]{1,0:T(4,128)S(1)} all-reduce(f32[4,128]{1,0:T(4,128)S(1)} %reduce_sum.81), channel_id=1, replica_groups=mesh['row'=8,'col'=16,'ch'=4] {'ch'}, use_global_device_ids=true, to_apply=%region_3.4 | all-reduce | flops 512 | bytes 4096 | tf_op jit(solution)/shard_map/psum | solution.py:107
  102.4 6.0 %psum.113 = f32[4,128]{1,0:T(4,128)S(1)} all-reduce(f32[4,128]{1,0:T(4,128)S(1)} %multiply_reduce_fusion.4), channel_id=1, replica_groups=mesh['row'=8,'col'=16,'ch'=4] {'ch'}, use_global_device_ids=true, to_apply=%region_5.6 | all-reduce | flops 512 | bytes 4096 | tf_op jit(solution)/shard_map/psum | solution.py:109
  109.3 10.1 %all_gather.6 = bf16[256,512]{1,0:T(8,128)(2,1)S(1)} all-gather(bf16[64,512]{1,0:T(8,128)(2,1)S(1)} %bitcast.44), channel_id=1, replica_groups=mesh['row'=8,'col'=16,'ch'=4] {'ch'}, dimensions={0}, use_global_device_ids=true | all-gather | bytes 327680 | tf_op jit(solution)/shard_map/all_gather | solution.py:115
  119.6 1.1 fusion.8
  123.4 86.5 %all-reduce.10.cloned.1.call-done = (f32[256,256]{1,0:T(8,128)}, f32[256,256]{1,0:T(8,128)}) async-done(((f32[256,256]{1,0:T(8,128)}, f32[256,256]{1,0:T(8,128)}), (f32[256,256]{1,0:T(8,128)}, f32[256,256]{1,0:T(8,128)})) %all-reduce.10.cloned.1.call-update) | async-done | bytes 524304 | tf_op jit(solution)/shard_map/psum | solution.py:156
  210.3 1.0 copy.25
  211.4 1.0 copy.28
  213.1 7.8 %all-reduce.4 = (f32[4,128]{1,0:T(4,128)S(1)}, f32[4,128]{1,0:T(4,128)S(1)}) all-reduce(f32[4,128]{1,0:T(4,128)S(1)} %get-tuple-element.383, f32[4,128]{1,0:T(4,128)S(1)} %bitcast.48), channel_id=1, replica_groups=mesh['row'=8,'col'=16,'ch'=4] {'ch'}, use_global_device_ids=true, to_apply=%region_11.12 | all-reduce | flops 1024 | bytes 8192 | tf_op jit(solution)/shard_map/psum | solution.py:136
  221.1 50.7 %while.47 = (s32[]{:T(128)}, f32[64,49]{0,1:T(8,128)S(1)}, f32[64,10,134]{2,1,0:T(8,128)S(1)}, f32[64,4,128]{2,1,0:T(4,128)S(1)}, s32[]{:T(128)}, /*index=5*/s32...) while((s32[]{:T(128)}, f32[64,49]{0,1:T(8,128)S(1)}, f32[64,10,134]{2,1,0:T(8,128)S(1)}, ...), condition=%wide.region_16.17_spmd, body=%wide.region_14.16_spmd.sunk | while | flops 65492 | bytes 263208 | solution.py:90
  221.1 0.9 multiply_reduce_fusion.6
  222.2 0.9 multiply_reduce_fusion.6
  223.2 0.9 multiply_reduce_fusion.6
  227.3 0.9 multiply_reduce_fusion.6
  228.4 0.9 multiply_reduce_fusion.6
  229.4 0.9 multiply_reduce_fusion.6
  234.6 0.9 multiply_reduce_fusion.6
  235.6 0.9 multiply_reduce_fusion.6
  240.8 0.9 multiply_reduce_fusion.6
  241.8 0.9 multiply_reduce_fusion.6
  242.9 0.9 multiply_reduce_fusion.6
  247.0 0.9 multiply_reduce_fusion.6
  248.0 0.9 multiply_reduce_fusion.6
  249.1 0.9 multiply_reduce_fusion.6
  254.3 0.9 multiply_reduce_fusion.6
  255.3 0.9 multiply_reduce_fusion.6
  260.5 0.9 multiply_reduce_fusion.6
  261.5 0.9 multiply_reduce_fusion.6
  262.5 0.9 multiply_reduce_fusion.6
  266.7 0.9 multiply_reduce_fusion.6
  271.8 24.9 %all-reduce.2 = (f32[64,49]{0,1:T(8,128)S(1)}, f32[64]{0:T(128)S(1)}, f32[64]{0:T(128)S(1)}, f32[256]{0:T(256)S(1)}) all-reduce(f32[64,49]{0,1:T(8,128)S(1)} %get-tuple-element.351, f32[64]{0:T(128)S(1)} %get-tuple-element.382, f32[64]{0:T(128)S(1)} %get-tuple-element.384, ...), channel_id=1, replica_groups=mesh['row'=8,'col'=16,'ch'=4] {'row'}, use_global_device_ids=true, to_apply=%region_17.18 | all-reduce | flops 3520 | bytes 28160 | tf_op jit(solution)/shard_map/psum | solution.py:156
  296.7 47.9 %all-reduce = (f32[64,49]{0,1:T(8,128)S(1)}, f32[64]{0:T(128)S(1)}, f32[64]{0:T(128)S(1)}, f32[256]{0:T(256)S(1)}) all-reduce(f32[64,49]{0,1:T(8,128)S(1)} %get-tuple-element.416, f32[64]{0:T(128)S(1)} %get-tuple-element.417, f32[64]{0:T(128)S(1)} %get-tuple-element.418, ...), channel_id=1, replica_groups=mesh['row'=8,'col'=16,'ch'=4] {'col'}, use_global_device_ids=true, to_apply=%region_18.19 | all-reduce | flops 3520 | bytes 28160 | tf_op jit(solution)/shard_map/psum | solution.py:155
  345.8 12.7 %collective-permute-start.4 = (bf16[64,3,128]{2,1,0:T(4,128)(2,1)S(1)}, bf16[64,3,128]{2,1,0:T(4,128)(2,1)S(1)}, u32[]{:S(2)}, u32[]{:S(2)}) collective-permute-start(bf16[64,3,128]{2,1,0:T(4,128)(2,1)S(1)} %get-tuple-element.430), channel_id=1, source_target_pairs={{0,64},{64,128},{128,192},{192,256},{256,320},{320,384},{384,448},... | collective-permute-start | bytes 147464 | tf_op jit(solution)/shard_map/ppermute | solution.py:19
  358.5 3.2 collective-permute-start.5
  362.3 1.8 collective-permute-done.5
  364.4 1.8 collective-permute-start.6
  366.2 1.3 collective-permute-start.7
  368.0 3.5 collective-permute-done.6
  371.5 4.1 collective-permute-done.7
  376.4 57.9 %while.49 = (s32[]{:T(128)}, f32[64,4,128]{2,1,0:T(4,128)S(1)}, f32[64,49]{0,1:T(8,128)}, f32[64,10,134]{2,1,0:T(8,128)S(1)}, s32[]{:T(128)}, /*index=5*/s32[]{:...) while((s32[]{:T(128)}, f32[64,4,128]{2,1,0:T(4,128)S(1)}, ...), condition=%wide.region_13.14_spmd.clone, body=%wide.region_12.13_spmd.clone.sunk | while | flops 98327 | bytes 394322 | solution.py:74
  435.0 1.9 broadcast_multiply_fusion
  436.8 1.0 copy.26
  (338 shorter events, 152.2 us)
Async XLA Ops:
  8.0 112.7 %copy-start = (bf16[256,256]{1,0:T(8,128)(2,1)S(1)}, bf16[256,256]{1,0:T(8,128)(2,1)}, u32[]{:S(2)}) copy-start(bf16[256,256]{1,0:T(8,128)(2,1)} %param.20) | copy-start | bytes 393220
  8.0 11.1 %copy-start.3 = (bf16[64,4,128]{2,1,0:T(4,128)(2,1)S(1)}, bf16[64,4,128]{2,1,0:T(4,128)(2,1)}, u32[]{:S(2)}) copy-start(bf16[64,4,128]{2,1,0:T(4,128)(2,1)} %param.21) | copy-start | bytes 196612
  8.0 201.9 %all-reduce.10.cloned.1.call-start = ((), (), s32[]{:S(2)}) async-start(), calls=%async_computation.5 | async-start | bytes 1048576 | tf_op jit(solution)/shard_map/psum | solution.py:156
  9.0 10.1 %collective-permute-start = (bf16[64,3,128]{2,1,0:T(4,128)(2,1)S(1)}, bf16[64,3,128]{2,1,0:T(4,128)(2,1)S(1)}, u32[]{:S(2)}, u32[]{:S(2)}) collective-permute-start(bf16[64,3,128]{2,1,0:T(4,128)(2,1)S(1)} %get-tuple-element.432), channel_id=1, source_target_pairs={{0,64},{64,128},{128,192},{192,256},{256,320},{320,384},{384,448},... | collective-permute-start | bytes 147464 | tf_op jit(solution)/shard_map/ppermute | solution.py:19
  13.6 6.3 %collective-permute-start.1 = (bf16[64,3,128]{2,1,0:T(4,128)(2,1)S(1)}, bf16[64,3,128]{2,1,0:T(4,128)(2,1)S(1)}, u32[]{:S(2)}, u32[]{:S(2)}) collective-permute-start(bf16[64,3,128]{2,1,0:T(4,128)(2,1)S(1)} %get-tuple-element.433), channel_id=1, source_target_pairs={{64,0},{128,64},{192,128},{256,192},{320,256},{384,320},{448,384},... | collective-permute-start | bytes 147464 | tf_op jit(solution)/shard_map/ppermute | solution.py:20
  19.1 0.9 copy-start.1
  20.3 15.5 %collective-permute-start.2 = (bf16[64,10,3]{2,1,0:T(8,128)(2,1)S(1)}, bf16[64,10,3]{2,1,0:T(8,128)(2,1)S(1)}, u32[]{:S(2)}, u32[]{:S(2)}) collective-permute-start(bf16[64,10,3]{2,1,0:T(8,128)(2,1)S(1)} %get-tuple-element.428), channel_id=1, source_target_pairs={{0,4},{4,8},{8,12},{12,16},{16,20},{20,24},{24,28},{28,32},{32,36}... | collective-permute-start | bytes 11528 | tf_op jit(solution)/shard_map/ppermute | solution.py:19
  23.1 12.7 %collective-permute-start.3 = (bf16[64,10,3]{2,1,0:T(8,128)(2,1)S(1)}, bf16[64,10,3]{2,1,0:T(8,128)(2,1)S(1)}, u32[]{:S(2)}, u32[]{:S(2)}) collective-permute-start(bf16[64,10,3]{2,1,0:T(8,128)(2,1)S(1)} %get-tuple-element.429), channel_id=1, source_target_pairs={{4,0},{8,4},{12,8},{16,12},{20,16},{24,20},{28,24},{32,28},{36,32}... | collective-permute-start | bytes 11528 | tf_op jit(solution)/shard_map/ppermute | solution.py:20
  108.4 0.7 copy-start.4
  108.4 0.7 copy-start.5
  109.3 10.1 %copy-start.2 = (bf16[256,256]{1,0:T(8,128)(2,1)S(1)}, bf16[256,256]{1,0:T(8,128)(2,1)}, u32[]{:S(2)}) copy-start(bf16[256,256]{1,0:T(8,128)(2,1)} %param.18) | copy-start | bytes 393220
  122.1 89.2 %reduce-scatter.9.cloned.1.call-start = ((), (), s32[]{:S(2)}) async-start(), calls=%async_computation.3 | async-start | bytes 327680
  123.3 311.6 %all-reduce.8.cloned.1.call-start = ((), (), s32[]{:S(2)}) async-start(), calls=%async_computation.4 | async-start | bytes 1048576 | tf_op jit(solution)/shard_map/psum | solution.py:155
  209.9 226.9 %reduce-scatter.7.cloned.1.call-start = ((), (), s32[]{:S(2)}) async-start(), calls=%async_computation.2 | async-start | bytes 655360
  345.8 16.5 %collective-permute-start.4 = (bf16[64,3,128]{2,1,0:T(4,128)(2,1)S(1)}, bf16[64,3,128]{2,1,0:T(4,128)(2,1)S(1)}, u32[]{:S(2)}, u32[]{:S(2)}) collective-permute-start(bf16[64,3,128]{2,1,0:T(4,128)(2,1)S(1)} %get-tuple-element.430), channel_id=1, source_target_pairs={{0,64},{64,128},{128,192},{192,256},{256,320},{320,384},{384,448},... | collective-permute-start | bytes 147464 | tf_op jit(solution)/shard_map/ppermute | solution.py:19
  358.5 5.6 %collective-permute-start.5 = (bf16[64,3,128]{2,1,0:T(4,128)(2,1)S(1)}, bf16[64,3,128]{2,1,0:T(4,128)(2,1)S(1)}, u32[]{:S(2)}, u32[]{:S(2)}) collective-permute-start(bf16[64,3,128]{2,1,0:T(4,128)(2,1)S(1)} %get-tuple-element.431), channel_id=1, source_target_pairs={{64,0},{128,64},{192,128},{256,192},{320,256},{384,320},{448,384},... | collective-permute-start | bytes 147464 | tf_op jit(solution)/shard_map/ppermute | solution.py:20
  364.4 7.1 %collective-permute-start.6 = (bf16[64,10,3]{2,1,0:T(8,128)(2,1)S(1)}, bf16[64,10,3]{2,1,0:T(8,128)(2,1)S(1)}, u32[]{:S(2)}, u32[]{:S(2)}) collective-permute-start(bf16[64,10,3]{2,1,0:T(8,128)(2,1)S(1)} %get-tuple-element.426), channel_id=1, source_target_pairs={{0,4},{4,8},{8,12},{12,16},{16,20},{20,24},{24,28},{28,32},{32,36}... | collective-permute-start | bytes 11528 | tf_op jit(solution)/shard_map/ppermute | solution.py:19
  366.2 9.4 %collective-permute-start.7 = (bf16[64,10,3]{2,1,0:T(8,128)(2,1)S(1)}, bf16[64,10,3]{2,1,0:T(8,128)(2,1)S(1)}, u32[]{:S(2)}, u32[]{:S(2)}) collective-permute-start(bf16[64,10,3]{2,1,0:T(8,128)(2,1)S(1)} %get-tuple-element.427), channel_id=1, source_target_pairs={{4,0},{8,4},{12,8},{16,12},{20,16},{24,20},{28,24},{32,28},{36,32}... | collective-permute-start | bytes 11528 | tf_op jit(solution)/shard_map/ppermute | solution.py:20
Sparse Core Ops, SparseCore 0:
  122.3 87.5 all-reduce.9
  212.3 129.1 all-reduce.7
Sparse Core Ops, SparseCore 1:
  126.0 39.0 reduce-scatter.8
  213.2 27.6 reduce-scatter.6
